TPU v7x, 32 devices: a whole 2x2x4 slice. The times are simulated.
32 devices in a mesh: tower: 4 (over y, x), rank: 8 (over z, core).
Axes of the slice: x: 2, y: 2, z: 4, core: 2. Of those that a mesh axis runs over, the one named last changes fastest.
Arguments:
- pooled: bfloat16 [2, 2048, 1024], P(None, ('tower', 'rank')), may hold values from -8 to 8
- feature_order: int32 [4, 4], P('tower'), may hold values from 0 to 3, as said below
- cross_weight: bfloat16 [4, 3, 512, 512], P('tower'), may hold values from -0.25 to 0.25
- cross_bias: float32 [4, 3, 512], P('tower'), may hold values from -3 to 3
- compress_weight: bfloat16 [4, 128, 512], P('tower'), may hold values from -0.25 to 0.25
- norm_gain: float32 [4, 128], P('tower'), may hold values from 0.1 to 1.9
- mlp_weight: bfloat16 [4096, 512], P(('tower', 'rank')), may hold values from -0.25 to 0.25
- mlp_bias: bfloat16 [4096], P(('tower', 'rank')), may hold values from -3 to 3
- out_weight: bfloat16 [4096], P(('tower', 'rank')), may hold values from -0.09375 to 0.09375
Outputs:
- logits: float32 [2, 8, 128], P(None, 'rank', 'tower')
Inputs may be any that keep to these rules, and one draw needn't show every extreme that they name: `feature_order`: each row is an ordering of 0 to 3.
All inputs are finite; a program needn't handle non-finite values.
Results may differ from a plain program's by a relative error of at most 0.0076.
Values may be sent and summed in bfloat16 or wider, within the bound.
A program may use at most 64 MiB of HBM per device.

v0:
```python
import jax
import jax.numpy as jnp
from jax import lax
from jax.sharding import PartitionSpec as P

E = 128
CD = 128
epsilon = 1e-06


def tower_block(first, weights, biases, compress, gain):
    first_f = first.astype(jnp.float32)
    current = first
    for layer in range(weights.shape[0]):
        product = (
            jnp.dot(weights[layer], current, preferred_element_type=jnp.float32)
            + biases[layer][:, None]
        )
        current = (first_f * product + current.astype(jnp.float32)).astype(jnp.bfloat16)
    squeezed = jnp.dot(compress, current, preferred_element_type=jnp.float32)
    inverse_rms = lax.rsqrt(jnp.mean(squeezed * squeezed, axis=0, keepdims=True) + epsilon)
    return (squeezed * inverse_rms * gain[:, None]).astype(jnp.bfloat16)


def interact(joined):
    samples_now = joined.shape[1]
    values_f = joined.astype(jnp.float32).reshape(-1, CD, samples_now)
    gram = jnp.einsum("tck,uck->tuk", values_f, values_f, precision=lax.Precision.HIGHEST) / CD
    mixed = values_f + jnp.einsum("tuk,uck->tck", gram, values_f, precision=lax.Precision.HIGHEST)
    return mixed.reshape(-1, samples_now).astype(jnp.bfloat16)


def logit_terms(hidden_rows, hidden_bias, hidden_out, features):
    hidden = (
        jnp.dot(hidden_rows, features, preferred_element_type=jnp.float32)
        + hidden_bias.astype(jnp.float32)[:, None]
    )
    return jnp.sum(
        jax.nn.relu(hidden) * hidden_out.astype(jnp.float32)[:, None], axis=0, keepdims=True
    )


def on_device(
    pooled,
    feature_order,
    cross_weight,
    cross_bias,
    compress_weight,
    norm_gain,
    mlp_weight,
    mlp_bias,
    out_weight,
):
    micro_count = pooled.shape[0]
    arriving = [
        lax.all_to_all(pooled[batch], "rank", split_axis=1, concat_axis=0, tiled=True)
        for batch in range(micro_count)
    ]
    hidden_rows, hidden_bias, hidden_out = (
        lax.all_gather(mlp_weight, "rank", axis=0, tiled=True),
        lax.all_gather(mlp_bias, "rank", axis=0, tiled=True),
        lax.all_gather(out_weight, "rank", axis=0, tiled=True),
    )
    results = []
    for batch in range(micro_count):
        arrived = arriving[batch]
        samples_here = arrived.shape[1]
        first = jnp.take(arrived.reshape(-1, E, samples_here), feature_order[0], axis=0).reshape(
            -1, samples_here
        )
        compressed = tower_block(
            first, cross_weight[0], cross_bias[0], compress_weight[0], norm_gain[0]
        )
        all_towers = lax.all_gather(compressed, "tower", axis=0, tiled=True)
        partial_value = logit_terms(hidden_rows, hidden_bias, hidden_out, interact(all_towers))
        logit_row = lax.psum_scatter(partial_value, "tower", scatter_dimension=1, tiled=True)
        results.append(logit_row)
    return jnp.stack(results)


def solution(mesh):
    return jax.shard_map(
        on_device,
        mesh=mesh,
        in_specs=(
            P(None, ("tower", "rank"), None),
            P("tower", None),
            P("tower", None, None, None),
            P("tower", None, None),
            P("tower", None, None),
            P("tower", None),
            P(("tower", "rank"), None),
            P(("tower", "rank")),
            P(("tower", "rank")),
        ),
        out_specs=P(None, "rank", "tower"),
        check_vma=False,
    )
```

profile of v0, /device:TPU:0, one launch (start us, length us, event | category | flops | bytes accessed | tf_op | source)
XLA Modules:
  0.0 129.5 jit_solution(2807232870646016834)
XLA Ops:
  6.5 1.0 slice_bitcast_fusion.1
  7.6 0.7 copy.34
  8.3 6.4 %all-to-all-start = ((bf16[64,8,128]{2,0,1:T(8,128)(2,1)}), bf16[64,8,128]{2,0,1:T(8,128)(2,1)S(1)}, u32[]{:S(2)}, u32[]{:S(2)}) async-start(bf16[64,8,128]{2,0,1:T(8,128)(2,1)} %copy.34), calls=%async_computation | async-start | bytes 262144 | tf_op jit(solution)/shard_map/all_to_all | solution.py:56
  14.7 0.7 all-gather.4.cloned.1.call-update
  15.4 0.7 compare_select_fusion
  16.1 0.7 copy.41
  16.8 4.6 %all-to-all-done = bf16[64,8,128]{2,0,1:T(8,128)(2,1)S(1)} async-done(((bf16[64,8,128]{2,0,1:T(8,128)(2,1)}), bf16[64,8,128]{2,0,1:T(8,128)(2,1)S(1)}, u32[]{:S(2)}, u32[]{:S(2)}) %all-to-all-start) | async-done | bytes 131104 | tf_op jit(solution)/shard_map/all_to_all | solution.py:56
  21.4 3.4 %all-to-all-start.1 = ((bf16[64,8,128]{2,0,1:T(8,128)(2,1)}), bf16[64,8,128]{2,0,1:T(8,128)(2,1)S(1)}, u32[]{:S(2)}, u32[]{:S(2)}) async-start(bf16[64,8,128]{2,0,1:T(8,128)(2,1)} %copy.41), calls=%async_computation.1 | async-start | bytes 262144 | tf_op jit(solution)/shard_map/all_to_all | solution.py:56
  24.8 12.2 %all-gather = bf16[8,1,128]{2,1,0:T(2,128)(2,1)S(1)} all-gather(bf16[1,1,128]{2,1,0:T(2,128)(2,1)S(1)} %bitcast.203), channel_id=1, replica_groups=mesh['tower'=4,'rank'=8] {'rank'}, dimensions={0}, use_global_device_ids=true | all-gather | bytes 2304 | tf_op jit(solution)/shard_map/all_gather | solution.py:61
  37.1 10.3 %all-gather.1 = bf16[8,1,128]{2,1,0:T(2,128)(2,1)S(1)} all-gather(bf16[1,1,128]{2,1,0:T(2,128)(2,1)S(1)} %bitcast.204), channel_id=1, replica_groups=mesh['tower'=4,'rank'=8] {'rank'}, dimensions={0}, use_global_device_ids=true | all-gather | bytes 2304 | tf_op jit(solution)/shard_map/all_gather | solution.py:62
  47.4 0.6 gather_fusion
  48.0 0.6 gather_fusion.1
  51.4 8.5 %all_gather.15 = bf16[512,128]{1,0:T(8,128)(2,1)S(1)} all-gather(bf16[128,128]{1,0:T(8,128)(2,1)S(1)} %get-tuple-element.11), channel_id=1, replica_groups=mesh['tower'=4,'rank'=8] {'tower'}, dimensions={0}, use_global_device_ids=true | all-gather | bytes 163840 | tf_op jit(solution)/shard_map/all_gather | solution.py:74
  60.0 8.5 %all_gather.19 = bf16[512,128]{1,0:T(8,128)(2,1)S(1)} all-gather(bf16[128,128]{1,0:T(8,128)(2,1)S(1)} %get-tuple-element.12), channel_id=1, replica_groups=mesh['tower'=4,'rank'=8] {'tower'}, dimensions={0}, use_global_device_ids=true | all-gather | bytes 163840 | tf_op jit(solution)/shard_map/all_gather | solution.py:74
  69.2 0.7 fusion.28
  69.9 0.7 fusion.29
  70.6 1.9 %fusion.5 = f32[128]{0:T(128)S(1)} fusion(bf16[1024,512]{1,0:T(8,128)(2,1)} %all-gather.4.cloned.1.call-done, f32[1024]{0:T(1024)S(1)} %bitcast.190, f32[1024]{0:T(1024)S(1)} %bitcast.188, bf16[16,8,4,128]{3,2,1,0:T(4,128)(2,1)S(1)} %bitcast.185), kind=kOutput, calls=%fused_computation.9 | convolution fusion | flops 134741888 | bytes 1188352 | tf_op jit(solution)/shard_map/dot_general | solution.py:35
  72.5 0.8 copy.52
  73.9 0.7 copy.54
  74.7 20.1 %reduce-scatter.7.cloned.1.call-done = f32[32,1]{1,0:T(8,128)} async-done(((f32[128,1]{1,0:T(8,128)}), f32[32,1]{1,0:T(8,128)}) %reduce-scatter.7.cloned.1.call-update) | async-done | bytes 144
  94.7 0.8 copy.53
  95.5 26.0 %reduce-scatter.9.cloned.1.call-done = f32[32,1]{1,0:T(8,128)} async-done(((f32[128,1]{1,0:T(8,128)}), f32[32,1]{1,0:T(8,128)}) %reduce-scatter.9.cloned.1.call-update) | async-done | bytes 144
  121.6 0.8 copy.55
  122.4 0.6 pad_maximum_fusion
  (46 shorter events, 4.4 us)
Async XLA Ops:
  6.5 43.4 %copy-start = (bf16[1,128,512]{2,1,0:T(8,128)(2,1)S(1)}, bf16[1,128,512]{2,1,0:T(8,128)(2,1)}, u32[]{:S(2)}) copy-start(bf16[1,128,512]{2,1,0:T(8,128)(2,1)} %param.15) | copy-start | bytes 393220
  6.5 10.2 %copy-start.7 = (s32[1,4]{1,0:T(1,128)S(1)}, s32[1,4]{1,0:T(1,128)}, u32[]{:S(2)}) copy-start(s32[1,4]{1,0:T(1,128)} %param.12) | copy-start | bytes 52
  6.5 18.3 %copy-start.3 = (bf16[128]{0:T(256)(128)(2,1)S(1)}, bf16[128]{0:T(256)(128)(2,1)}, u32[]{:S(2)}) copy-start(bf16[128]{0:T(256)(128)(2,1)} %param.18) | copy-start | bytes 772
  6.5 30.5 %copy-start.4 = (bf16[128]{0:T(256)(128)(2,1)S(1)}, bf16[128]{0:T(256)(128)(2,1)}, u32[]{:S(2)}) copy-start(bf16[128]{0:T(256)(128)(2,1)} %param.19) | copy-start | bytes 772
  6.5 40.9 %copy-start.1 = (f32[1,3,512]{2,0,1:T(1,128)S(1)}, f32[1,3,512]{2,0,1:T(1,128)}, u32[]{:S(2)}) copy-start(f32[1,3,512]{2,0,1:T(1,128)} %param.14) | copy-start | bytes 18436
  7.6 41.4 %copy-start.5 = (bf16[1,3,512,512]{3,2,1,0:T(8,128)(2,1)S(1)}, bf16[1,3,512,512]{3,2,1,0:T(8,128)(2,1)}, u32[]{:S(2)}) copy-start(bf16[1,3,512,512]{3,2,1,0:T(8,128)(2,1)} %param.13) | copy-start | bytes 4718596
  8.3 13.1 %all-to-all-start = ((bf16[64,8,128]{2,0,1:T(8,128)(2,1)}), bf16[64,8,128]{2,0,1:T(8,128)(2,1)S(1)}, u32[]{:S(2)}, u32[]{:S(2)}) async-start(bf16[64,8,128]{2,0,1:T(8,128)(2,1)} %copy.34), calls=%async_computation | async-start | bytes 262144 | tf_op jit(solution)/shard_map/all_to_all | solution.py:56
  14.6 56.0 %all-gather.4.cloned.1.call-start = ((), (), s32[]{:S(2)}) async-start(), calls=%async_computation.4 | async-start | bytes 1179648 | tf_op jit(solution)/shard_map/all_gather | solution.py:60
  21.4 26.6 %all-to-all-start.1 = ((bf16[64,8,128]{2,0,1:T(8,128)(2,1)}), bf16[64,8,128]{2,0,1:T(8,128)(2,1)S(1)}, u32[]{:S(2)}, u32[]{:S(2)}) async-start(bf16[64,8,128]{2,0,1:T(8,128)(2,1)} %copy.41), calls=%async_computation.1 | async-start | bytes 262144 | tf_op jit(solution)/shard_map/all_to_all | solution.py:56
  24.8 70.0 %reduce-scatter.7.cloned.1.call-start = ((), (), s32[]{:S(2)}) async-start(), calls=%async_computation.5 | async-start | bytes 81920
  50.0 1.3 %copy-start.2 = (f32[1,128]{1,0:T(1,128)S(1)}, f32[1,128]{1,0:T(1,128)}, u32[]{:S(2)}) copy-start(f32[1,128]{1,0:T(1,128)} %param.16) | copy-start | bytes 1540
  70.6 2.7 %copy-start.6 = (bf16[1024,512]{1,0:T(8,128)(2,1)S(1)}, bf16[1024,512]{1,0:T(8,128)(2,1)}, u32[]{:S(2)}) copy-start(bf16[1024,512]{1,0:T(8,128)(2,1)} %all-gather.4.cloned.1.call-done) | copy-start | bytes 3145732
  73.3 48.3 %reduce-scatter.9.cloned.1.call-start = ((), (), s32[]{:S(2)}) async-start(), calls=%async_computation.6 | async-start | bytes 81920
Sparse Core Ops, SparseCore 0:
  17.1 25.6 all-gather.3
  73.4 21.3 reduce-scatter.6
  97.5 24.0 reduce-scatter.8
where the time goes:
time: 130 us; the launch traced here: 129 us
  waiting for transfers between devices  51.5 us (40%)
  blocking collectives  39.5 us (30%)
  between operations  13.4 us (10%)
  starting transfers between devices  9.84 us (8%)
  local copies, waits for them, and re-layouts  7.22 us (6%)
  matrix products  6.64 us (5%)
  other arithmetic  1.44 us (1%)
    unnamed x5, waiting for transfers between devices  46.8 us
    all_gather x2, blocking collectives, on_device(): all_towers = lax.all_gather(compressed, 'tower', axis=0, tiled=True)  16.9 us
    all_gather x1, blocking collectives, on_device(): lax.all_gather(mlp_bias, 'rank', axis=0, tiled=True)  12.2 us
    all_gather x1, blocking collectives, on_device(): lax.all_gather(out_weight, 'rank', axis=0, tiled=True)  10.3 us
    all_to_all x2, starting transfers between devices, on_device(): lax.all_to_all(pooled[batch], 'rank', split_axis=1, concat_axis=0, tiled=...  9.72 us
    all_to_all x2, waiting for transfers between devices, on_device(): lax.all_to_all(pooled[batch], 'rank', split_axis=1, concat_axis=0, tiled=...  4.63 us
    unnamed x23, local copies, waits for them, and re-layouts  4.19 us
  transfers between devices with their start and end apart: 5, of which 3 were waited for; matrix products, arithmetic and copies ran while one was open for 7% of the time, Pallas kernels for 0%

commit v1 on v0

--- a/solution.py
+++ b/solution.py
@@ -6,6 +6,13 @@
 E = 128
 CD = 128
 epsilon = 1e-06
+
+
+def _fix_tokens(local_x):
+    met_up = jnp.stack(jnp.split(local_x, lax.axis_size("rank"), 1), 0)
+    b_now = lax.all_to_all(met_up, "rank", 0, 0)
+    spare = jnp.concatenate(b_now, 0)
+    return spare
 
 
 def tower_block(first, weights, biases, compress, gain):
@@ -52,10 +59,7 @@
     out_weight,
 ):
     micro_count = pooled.shape[0]
-    arriving = [
-        lax.all_to_all(pooled[batch], "rank", split_axis=1, concat_axis=0, tiled=True)
-        for batch in range(micro_count)
-    ]
+    arriving = [_fix_tokens(pooled[batch]) for batch in range(micro_count)]
     hidden_rows, hidden_bias, hidden_out = (
         lax.all_gather(mlp_weight, "rank", axis=0, tiled=True),
         lax.all_gather(mlp_bias, "rank", axis=0, tiled=True),

time: 130 us -> 137 us (1.054)
  local copies, waits for them, and re-layouts: 7.22 us -> 15.5 us
  waiting for transfers between devices: 51.5 us -> 46.9 us
  starting transfers between devices: 9.84 us -> 11.6 us
    unnamed x23 -> x32, local copies, waits for them, and re-layouts: 4.19 us -> 11.6 us
    all_to_all x2, waiting for transfers between devices: 4.63 us -> 0.01 us  [_fix_tokens(): b_now = lax.all_to_all(met_up, 'rank', 0, 0)]
    all_to_all x2, starting transfers between devices: 9.72 us -> 11.4 us  [_fix_tokens(): b_now = lax.all_to_all(met_up, 'rank', 0, 0)]
  transfers between devices with their start and end apart: 5 -> 5, of which waited for: 3 -> 2; matrix products, arithmetic and copies ran while one was open for 7% -> 11% of each run, Pallas kernels for 0% -> 0%
where the time goes in v1:
time: 137 us; the launch traced here: 136 us
  waiting for transfers between devices  46.9 us (34%)
  blocking collectives  40.2 us (29%)
  local copies, waits for them, and re-layouts  15.5 us (11%)
  between operations  13.3 us (10%)
  starting transfers between devices  11.6 us (8%)
  matrix products  6.64 us (5%)
  other arithmetic  2.1 us (2%)
    unnamed x5, waiting for transfers between devices  46.9 us
    all_gather x2, blocking collectives, on_device(): all_towers = lax.all_gather(compressed, 'tower', axis=0, tiled=True)  17 us
    all_gather x1, blocking collectives, on_device(): lax.all_gather(mlp_bias, 'rank', axis=0, tiled=True)  12.3 us
    unnamed x32, local copies, waits for them, and re-layouts  11.6 us
    all_to_all x2, starting transfers between devices, _fix_tokens(): b_now = lax.all_to_all(met_up, 'rank', 0, 0)  11.4 us
    all_gather x1, blocking collectives, on_device(): lax.all_gather(out_weight, 'rank', axis=0, tiled=True)  10.9 us
  transfers between devices with their start and end apart: 5, of which 2 were waited for; matrix products, arithmetic and copies ran while one was open for 11% of the time, Pallas kernels for 0%

profile of v1, /device:TPU:0, one launch (start us, length us, event | category | flops | bytes accessed | tf_op | source)
XLA Modules:
  0.0 136.3 jit_solution(3290781845319269937)
XLA Ops:
  6.5 1.1 slice_bitcast_fusion.1
  7.7 0.6 constant_dynamic-update-slice_fusion.15
  8.3 0.6 constant_dynamic-update-slice_fusion.14
  8.9 0.6 constant_dynamic-update-slice_fusion.13
  12.5 6.4 %all-to-all-start.1 = ((bf16[8,64,128]{2,1,0:T(8,128)(2,1)}), bf16[8,64,128]{2,1,0:T(8,128)(2,1)S(1)}, u32[]{:S(2)}, u32[]{:S(2)}) async-start(bf16[8,64,128]{2,1,0:T(8,128)(2,1)} %constant_dynamic-update-slice_fusion.8), calls=%async_computation.1 | async-start | bytes 262144 | tf_op jit(solution)/shard_map/all_to_all | solution.py:13
  18.9 0.7 all-gather.4.cloned.1.call-update
  19.6 0.7 compare_select_fusion
  20.8 0.6 constant_dynamic-update-slice_fusion.6
  22.7 0.6 constant_dynamic-update-slice_fusion.3
  24.5 0.7 compare_and_fusion
  25.8 5.1 %all-to-all-start = ((bf16[8,64,128]{2,1,0:T(8,128)(2,1)}), bf16[8,64,128]{2,1,0:T(8,128)(2,1)S(1)}, u32[]{:S(2)}, u32[]{:S(2)}) async-start(bf16[8,64,128]{2,1,0:T(8,128)(2,1)} %constant_dynamic-update-slice_fusion), calls=%async_computation | async-start | bytes 262144 | tf_op jit(solution)/shard_map/all_to_all | solution.py:13
  30.9 12.3 %all-gather = bf16[8,1,128]{2,1,0:T(2,128)(2,1)S(1)} all-gather(bf16[1,1,128]{2,1,0:T(2,128)(2,1)S(1)} %bitcast.257), channel_id=1, replica_groups=mesh['tower'=4,'rank'=8] {'rank'}, dimensions={0}, use_global_device_ids=true | all-gather | bytes 2304 | tf_op jit(solution)/shard_map/all_gather | solution.py:65
  43.2 10.9 %all-gather.1 = bf16[8,1,128]{2,1,0:T(2,128)(2,1)S(1)} all-gather(bf16[1,1,128]{2,1,0:T(2,128)(2,1)S(1)} %bitcast.258), channel_id=1, replica_groups=mesh['tower'=4,'rank'=8] {'rank'}, dimensions={0}, use_global_device_ids=true | all-gather | bytes 2304 | tf_op jit(solution)/shard_map/all_gather | solution.py:66
  58.1 8.6 %all_gather.15 = bf16[512,128]{1,0:T(8,128)(2,1)S(1)} all-gather(bf16[128,128]{1,0:T(8,128)(2,1)S(1)} %get-tuple-element.11), channel_id=1, replica_groups=mesh['tower'=4,'rank'=8] {'tower'}, dimensions={0}, use_global_device_ids=true | all-gather | bytes 163840 | tf_op jit(solution)/shard_map/all_gather | solution.py:78
  66.9 8.4 %all_gather.19 = bf16[512,128]{1,0:T(8,128)(2,1)S(1)} all-gather(bf16[128,128]{1,0:T(8,128)(2,1)S(1)} %get-tuple-element.12), channel_id=1, replica_groups=mesh['tower'=4,'rank'=8] {'tower'}, dimensions={0}, use_global_device_ids=true | all-gather | bytes 163840 | tf_op jit(solution)/shard_map/all_gather | solution.py:78
  76.0 0.7 fusion.28
  76.7 0.7 fusion.29
  77.4 1.9 %fusion.5 = f32[128]{0:T(128)S(1)} fusion(bf16[1024,512]{1,0:T(8,128)(2,1)} %all-gather.4.cloned.1.call-done, f32[1024]{0:T(1024)S(1)} %bitcast.244, f32[1024]{0:T(1024)S(1)} %bitcast.242, bf16[16,8,4,128]{3,2,1,0:T(4,128)(2,1)S(1)} %bitcast.239), kind=kOutput, calls=%fused_computation.9 | convolution fusion | flops 134741888 | bytes 1188352 | tf_op jit(solution)/shard_map/dot_general | solution.py:42
  79.3 0.7 copy.36
  80.7 0.7 copy.38
  81.5 20.1 %reduce-scatter.7.cloned.1.call-done = f32[32,1]{1,0:T(8,128)} async-done(((f32[128,1]{1,0:T(8,128)}), f32[32,1]{1,0:T(8,128)}) %reduce-scatter.7.cloned.1.call-update) | async-done | bytes 144
  101.5 0.8 copy.37
  102.3 26.1 %reduce-scatter.9.cloned.1.call-done = f32[32,1]{1,0:T(8,128)} async-done(((f32[128,1]{1,0:T(8,128)}), f32[32,1]{1,0:T(8,128)}) %reduce-scatter.9.cloned.1.call-update) | async-done | bytes 144
  128.4 0.8 copy.39
  (56 shorter events, 12.7 us)
Async XLA Ops:
  6.5 50.1 %copy-start = (bf16[1,128,512]{2,1,0:T(8,128)(2,1)S(1)}, bf16[1,128,512]{2,1,0:T(8,128)(2,1)}, u32[]{:S(2)}) copy-start(bf16[1,128,512]{2,1,0:T(8,128)(2,1)} %param.15) | copy-start | bytes 393220
  6.5 24.4 %copy-start.3 = (bf16[128]{0:T(256)(128)(2,1)S(1)}, bf16[128]{0:T(256)(128)(2,1)}, u32[]{:S(2)}) copy-start(bf16[128]{0:T(256)(128)(2,1)} %param.18) | copy-start | bytes 772
  6.5 36.7 %copy-start.4 = (bf16[128]{0:T(256)(128)(2,1)S(1)}, bf16[128]{0:T(256)(128)(2,1)}, u32[]{:S(2)}) copy-start(bf16[128]{0:T(256)(128)(2,1)} %param.19) | copy-start | bytes 772
  6.5 47.6 %copy-start.1 = (f32[1,3,512]{2,0,1:T(1,128)S(1)}, f32[1,3,512]{2,0,1:T(1,128)}, u32[]{:S(2)}) copy-start(f32[1,3,512]{2,0,1:T(1,128)} %param.14) | copy-start | bytes 18436
  6.5 49.1 %copy-start.5 = (bf16[1,3,512,512]{3,2,1,0:T(8,128)(2,1)S(1)}, bf16[1,3,512,512]{3,2,1,0:T(8,128)(2,1)}, u32[]{:S(2)}) copy-start(bf16[1,3,512,512]{3,2,1,0:T(8,128)(2,1)} %param.13) | copy-start | bytes 4718596
  12.5 13.3 %all-to-all-start.1 = ((bf16[8,64,128]{2,1,0:T(8,128)(2,1)}), bf16[8,64,128]{2,1,0:T(8,128)(2,1)S(1)}, u32[]{:S(2)}, u32[]{:S(2)}) async-start(bf16[8,64,128]{2,1,0:T(8,128)(2,1)} %constant_dynamic-update-slice_fusion.8), calls=%async_computation.1 | async-start | bytes 262144 | tf_op jit(solution)/shard_map/all_to_all | solution.py:13
  18.9 58.6 %all-gather.4.cloned.1.call-start = ((), (), s32[]{:S(2)}) async-start(), calls=%async_computation.4 | async-start | bytes 1179648 | tf_op jit(solution)/shard_map/all_gather | solution.py:64
  25.8 29.0 %all-to-all-start = ((bf16[8,64,128]{2,1,0:T(8,128)(2,1)}), bf16[8,64,128]{2,1,0:T(8,128)(2,1)S(1)}, u32[]{:S(2)}, u32[]{:S(2)}) async-start(bf16[8,64,128]{2,1,0:T(8,128)(2,1)} %constant_dynamic-update-slice_fusion), calls=%async_computation | async-start | bytes 262144 | tf_op jit(solution)/shard_map/all_to_all | solution.py:13
  30.8 70.7 %reduce-scatter.7.cloned.1.call-start = ((), (), s32[]{:S(2)}) async-start(), calls=%async_computation.5 | async-start | bytes 81920
  56.7 1.3 copy-start.2
  77.4 2.7 %copy-start.6 = (bf16[1024,512]{1,0:T(8,128)(2,1)S(1)}, bf16[1024,512]{1,0:T(8,128)(2,1)}, u32[]{:S(2)}) copy-start(bf16[1024,512]{1,0:T(8,128)(2,1)} %all-gather.4.cloned.1.call-done) | copy-start | bytes 3145732
  80.1 48.3 %reduce-scatter.9.cloned.1.call-start = ((), (), s32[]{:S(2)}) async-start(), calls=%async_computation.6 | async-start | bytes 81920
Sparse Core Ops, SparseCore 0:
  21.3 25.8 all-gather.3
  80.2 21.3 reduce-scatter.6
  104.3 24.0 reduce-scatter.8
